TPU v7x, 128 devices: a whole 4x4x4 slice. The times are simulated.
128 devices in a mesh: dp: 8 (over x, core), seq: 16 (over z, y).
Axes of the slice: x: 4, y: 4, z: 4, core: 2. Of those that a mesh axis runs over, the one named last changes fastest.
Arguments:
- tokens: bfloat16 [8, 12288, 2560], P('dp', 'seq'), may hold values from -6 to 6
- w_xbc: bfloat16 [2560, 2816], P(('dp', 'seq')), may hold values from -0.125 to 0.125
- conv_weight: float32 [4, 2816], replicated, may hold values from -3 to 3
- conv_bias: float32 [2816], replicated, may hold values from -2 to 2
- a_log: float32 [40], replicated, may hold values from -13 to -3
- dt_in: float32 [8, 40, 12288], P('dp', None, 'seq'), may hold values from -2 to 98304
- d_skip: float32 [40], replicated, may hold values from 0.5 to 1.5
- norm_gain: float32 [2560], replicated, may hold values from 0.25 to 1.75
Outputs:
- normed: bfloat16 [8, 12288, 2560], P('dp', 'seq')
All inputs are finite; a program needn't handle non-finite values.
Results may differ from a plain program's by a relative error of at most 0.012.
Values may be sent and summed in bfloat16 or wider, within the bound.
A program may use at most 128 MiB of HBM per device.

v0:
```python
import jax
import jax.numpy as jnp
from jax import lax
from jax.sharding import PartitionSpec as P

GROUP = 256


def passed_along(value, axis, by):
    length = lax.axis_size(axis)
    pairs = [(i, i + by) for i in range(length) if 0 <= i + by < length]
    return lax.ppermute(value, axis, pairs)


def prefix(value, axis, join, neutral):
    count, mine = (lax.axis_size(axis), lax.axis_index(axis))
    pieces = jax.tree.map(lambda part: lax.all_gather(part, axis), value)
    running = jax.tree.map(
        lambda part, zero: jnp.full_like(part, 0) + jnp.asarray(zero, part.dtype), value, neutral
    )

    def hop(position, running):
        longer = join(running, jax.tree.map(lambda part: part[position], pieces))
        return jax.tree.map(lambda new, old: jnp.where(position < mine, new, old), longer, running)

    return lax.fori_loop(0, count - 1, hop, running)


def block_state(x_block, b_block, dt_block, decay_block):
    heads = dt_block.shape[0]
    length = dt_block.shape[1]
    x_heads = x_block.astype(jnp.float32).reshape(length, heads, -1)
    cumul = jnp.cumsum(decay_block, axis=1)
    tail_weight = jnp.exp(cumul[:, -1:] - cumul) * dt_block
    weighted = tail_weight.T[:, :, None] * x_heads
    span_state = jnp.einsum(
        "jhp,jn->hpn", weighted, b_block.astype(jnp.float32), precision=lax.Precision.HIGH
    )
    return (span_state, cumul[:, -1])


def block_inner(x_block, b_block, c_block, dt_block, decay_block):
    heads = dt_block.shape[0]
    length = dt_block.shape[1]
    x_heads = x_block.astype(jnp.float32).reshape(length, heads, -1)
    cumul = jnp.cumsum(decay_block, axis=1)
    spread = cumul[:, :, None] - cumul[:, None, :]
    lower = jnp.arange(length)[:, None] >= jnp.arange(length)[None, :]
    decay_mat = jnp.exp(jnp.where(lower[None], spread, -jnp.inf))
    scores = jnp.dot(c_block, b_block.T, preferred_element_type=jnp.float32)
    mixing = decay_mat * scores[None] * dt_block[:, None, :]
    y_inner = jnp.einsum("hij,jhp->ihp", mixing, x_heads, precision=lax.Precision.HIGH)
    return (y_inner, cumul, x_heads)


def combine_carry(earlier, later):
    return (earlier[0] + later[0], jnp.exp(later[0])[:, None, None] * earlier[1] + later[1])


def local(tokens, w_xbc, conv_weight, conv_bias, a_log, dt_in, d_skip, norm_gain):
    token_rows = tokens[0]
    tok_count = token_rows.shape[0]
    heads = a_log.shape[0]
    width_x = norm_gain.shape[0]
    head_size = width_x // heads
    channels = w_xbc.shape[1]
    state_size = (channels - width_x) // 2
    kernel = conv_weight.shape[0]
    projected = jnp.dot(
        token_rows,
        lax.all_gather(w_xbc, ("dp", "seq"), axis=0, tiled=True),
        preferred_element_type=jnp.float32,
    )
    xbc = projected.astype(jnp.bfloat16)
    rim_rows = passed_along(xbc[tok_count - (kernel - 1) :], "seq", 1)
    padded = jnp.concatenate([rim_rows, xbc], axis=0)
    accum = conv_bias[None, :] + jnp.zeros((tok_count, channels), jnp.float32)
    for tap_index in range(kernel):
        accum = accum + conv_weight[tap_index][None, :] * padded[
            tap_index : tap_index + tok_count
        ].astype(jnp.float32)
    conv_out = jax.nn.silu(accum).astype(jnp.bfloat16)
    step_size = jax.nn.softplus(dt_in[0])
    log_decay = -jnp.exp(a_log)[:, None] * step_size
    blocks = tok_count // GROUP
    gain_heads = norm_gain.reshape(heads, head_size)[None]
    pieces = []
    own_state = jnp.zeros((heads, head_size, state_size), jnp.float32)
    own_decay = jnp.zeros((heads,), jnp.float32)
    for block_index in range(blocks):
        lo_row = block_index * GROUP
        block_rows = conv_out[lo_row : lo_row + GROUP]
        x_block = block_rows[:, :width_x]
        b_block = block_rows[:, width_x : width_x + state_size]
        c_block = block_rows[:, width_x + state_size :]
        dt_block = step_size[:, lo_row : lo_row + GROUP]
        decay_block = log_decay[:, lo_row : lo_row + GROUP]
        span_state, totals = block_state(x_block, b_block, dt_block, decay_block)
        own_state = jnp.exp(totals)[:, None, None] * own_state + span_state
        own_decay = own_decay + totals
        pieces.append((x_block, b_block, c_block, dt_block, decay_block, span_state, totals))
    identity = (jnp.zeros_like(own_decay), jnp.zeros_like(own_state))
    earlier_decay, incoming = prefix((own_decay, own_state), "seq", combine_carry, identity)
    state = incoming
    outputs = []
    for block_index in range(blocks):
        x_block, b_block, c_block, dt_block, decay_block, span_state, totals = pieces[block_index]
        y_inner, cumul, x_heads = block_inner(x_block, b_block, c_block, dt_block, decay_block)
        from_state = jnp.einsum(
            "in,hpn->ihp", c_block.astype(jnp.float32), state, precision=lax.Precision.HIGH
        )
        ssd = y_inner + jnp.exp(cumul).T[:, :, None] * from_state + d_skip[None, :, None] * x_heads
        mean_sq = jnp.mean(ssd * ssd, axis=-1, keepdims=True)
        scaled = ssd * lax.rsqrt(mean_sq + 1e-05) * gain_heads
        outputs.append(scaled.reshape(GROUP, width_x).astype(jnp.bfloat16))
        state = jnp.exp(totals)[:, None, None] * state + span_state
    return jnp.concatenate(outputs, axis=0)[None]


def solution(mesh):
    return jax.shard_map(
        local,
        mesh=mesh,
        in_specs=(
            P("dp", "seq", None),
            P(("dp", "seq"), None),
            P(),
            P(),
            P(),
            P("dp", None, "seq"),
            P(),
            P(),
        ),
        out_specs=P("dp", "seq", None),
        check_vma=False,
    )
```

profile of v0, /device:TPU:1, one launch (start us, length us, event | category | flops | bytes accessed | tf_op | source)
XLA Modules:
  0.0 367.9 jit_solution(12167026714870173154)
XLA Ops:
  6.5 0.7 all-gather.8.cloned.1.call-update
  8.0 1.0 compare_select_fusion
  12.4 0.8 fusion.91
  13.2 81.4 %all-gather.8.cloned.1.call-done = bf16[128,20,2816]{2,1,0:T(8,128)(2,1)} async-done(((bf16[1,20,2816]{2,1,0:T(8,128)(2,1)}), bf16[128,20,2816]{2,1,0:T(8,128)(2,1)}) %all-gather.8.cloned.1.call-update) | async-done | bytes 14417936 | tf_op jit(solution)/shard_map/all_gather | solution.py:71
  94.6 20.5 %reshape.252 = bf16[2560,2816]{1,0:T(8,128)(2,1)} reshape(bf16[128,20,2816]{2,1,0:T(8,128)(2,1)} %all-gather.8.cloned.1.call-done) | data formatting | bytes 28835840
  115.1 16.4 %convolution_convert_fusion = bf16[768,2816]{1,0:T(8,128)(2,1)S(1)} fusion(bf16[2560,2816]{1,0:T(8,128)(2,1)} %reshape.252, bf16[1,768,2560]{2,1,0:T(8,128)(2,1)} %param.10), kind=kOutput, calls=%fused_computation.42 | convolution fusion | flops 11075125248 | bytes 22675456 | tf_op jit(solution)/shard_map/dot_general | solution.py:69
  131.6 3.1 collective-permute-start
  134.9 0.7 collective-permute-done
  135.6 6.3 %multiply_convert_fusion = bf16[768,2816]{1,0:T(8,128)(2,1)S(1)} fusion(bf16[768,2816]{1,0:T(8,128)(2,1)S(1)} %convolution_convert_fusion, bf16[3,2816]{1,0:T(4,128)(2,1)S(1)} %collective-permute-done, f32[2816]{0:T(1024)S(1)} %get-tuple-element.120, f32[2816]{0:T(1024)S(1)} %get-tuple-element.121, f32[2816]{0:T(1024)S(1)} %get-tuple-element.119, ...), kind=kLoop, calls=%fused_computation.21 | loop fusion | flops 56229888 | bytes 8723968 | tf_op jit(solution)/shard_map/convert_element_type | solution.py:82
  141.9 2.0 fusion.90
  143.9 0.8 copy-done
  144.8 1.6 copy.33
  146.4 2.9 copy.40
  149.3 1.5 copy.41
  150.8 1.8 fusion.40
  152.6 1.7 fusion.42
  154.4 1.0 copy-done.1
  155.4 2.9 fusion.52
  159.8 34.8 %all-reduce = f32[640]{0:T(1024)S(1)} all-reduce(f32[640]{0:T(1024)S(1)} %dynamic-update-slice), channel_id=2, replica_groups=mesh['dp'=8,'seq'=16] {'seq'}, use_global_device_ids=true, to_apply=%add | all-reduce | flops 640 | bytes 5120
  195.9 1.1 fusion.73
  197.0 1.1 fusion.76
  198.0 1.1 fusion.83
  199.1 93.6 %all-gather.6.cloned.1.call-done = f32[640,64,128]{2,1,0:T(8,128)} async-done(((f32[40,64,128]{2,1,0:T(8,128)}), f32[640,64,128]{2,1,0:T(8,128)}) %all-gather.6.cloned.1.call-update) | async-done | bytes 20971536 | tf_op jit(solution)/shard_map/all_gather | solution.py:17
  292.7 35.1 %while.14 = (s32[]{:T(128)}, f32[40,64,128]{2,1,0:T(8,128)S(1)}, s32[]{:T(128)}, f32[16,40]{1,0:T(8,128)}, f32[16,40,64,128]{3,2,1,0:T(8,128)}, /*index=5*/s32[]{:T(128)}, s32[]{:T(128)}) while((s32[]{:T(128)}, f32[40,64,128]{2,1,0:T(8,128)S(1)}, s32[]{:T(128)}, f32[16,40]{1,0:T(8,128)}, f32[16,40,64,128]{3,2,1,0:T(8,128)}, ...), condition=%wide.region_7.8_spmd.clone, body=%wide.region_6.7_spmd.clone.sunk | while | flops 1310724 | bytes 3932745 | solution.py:26
  293.4 1.6 fusion.99
  295.0 0.7 exponential_bitcast_fusion.5
  295.7 1.6 fusion.99
  297.4 0.7 exponential_bitcast_fusion.5
  298.0 1.6 fusion.99
  299.7 0.7 exponential_bitcast_fusion.5
  300.4 1.6 fusion.99
  302.0 0.7 exponential_bitcast_fusion.5
  302.7 1.6 fusion.99
  304.3 0.7 exponential_bitcast_fusion.5
  305.0 1.6 fusion.99
  306.7 0.7 exponential_bitcast_fusion.5
  307.4 1.6 fusion.99
  309.0 0.7 exponential_bitcast_fusion.5
  309.7 1.6 fusion.99
  311.3 0.7 exponential_bitcast_fusion.5
  312.0 1.6 fusion.99
  313.6 0.7 exponential_bitcast_fusion.5
  314.3 1.6 fusion.99
  316.0 0.7 exponential_bitcast_fusion.5
  316.7 1.6 fusion.99
  318.3 0.7 exponential_bitcast_fusion.5
  319.0 1.6 fusion.99
  320.6 0.7 exponential_bitcast_fusion.5
  321.3 1.6 fusion.99
  323.0 0.7 exponential_bitcast_fusion.5
  323.7 1.6 fusion.99
  325.3 0.7 exponential_bitcast_fusion.5
  326.0 1.6 fusion.99
  327.8 2.2 fusion.53
  330.0 1.7 fusion.60
  331.8 1.8 fusion.70
  333.7 5.3 %multiply_reduce_fusion = (f32[256,40]{0,1:T(8,128)S(1)}, f32[256,40,64]{0,2,1:T(8,128)S(1)}) fusion(bf16[256,40,64]{0,2,1:T(8,128)(2,1)S(1)} %bitcast.140, f32[40]{0:T(128)S(1)} %copy-done.21, f32[256,40,64]{0,2,1:T(8,128)S(1)} %fusion.53, f32[256,40]{0,1:T(8,128)S(1)} %copy-done.16, f32[40,256]{1,0:T(8,128)S(1)} %copy-done.15, ...), kind=kOutput, calls=%fused_computation.64 | convolution fusion | flops 1021696000 | bytes 7045280 | tf_op jit(solution)/shard_map/hij,jhp->ihp/dot_general | solution.py:52
  339.1 5.5 %multiply_reduce_fusion.1 = (f32[256,40]{0,1:T(8,128)S(1)}, f32[256,40,64]{0,2,1:T(8,128)S(1)}) fusion(bf16[256,40,64]{0,2,1:T(8,128)(2,1)S(1)} %bitcast.138, f32[40]{0:T(128)S(1)} %copy-done.21, f32[256,40,64]{0,2,1:T(8,128)S(1)} %fusion.60, f32[256,40]{0,1:T(8,128)S(1)} %copy-done.14, f32[40,256]{1,0:T(8,128)S(1)} %copy-done.13, ...), kind=kOutput, calls=%fused_computation.66 | convolution fusion | flops 1021696000 | bytes 7045280 | tf_op jit(solution)/shard_map/hij,jhp->ihp/dot_general | solution.py:52
  344.6 5.2 %multiply_reduce_fusion.2 = (f32[256,40]{0,1:T(8,128)S(1)}, f32[256,40,64]{0,2,1:T(8,128)S(1)}) fusion(bf16[256,40,64]{0,2,1:T(8,128)(2,1)S(1)} %bitcast.136, f32[40]{0:T(128)S(1)} %copy-done.21, f32[256,40,64]{0,2,1:T(8,128)S(1)} %fusion.70, f32[256,40]{0,1:T(8,128)S(1)} %copy-done.12, f32[40,256]{1,0:T(8,128)S(1)} %copy-done.11, ...), kind=kOutput, calls=%fused_computation.68 | convolution fusion | flops 1021696000 | bytes 7045280 | tf_op jit(solution)/shard_map/hij,jhp->ihp/dot_general | solution.py:52
  349.9 2.2 multiply_convert_fusion.3
  352.1 2.4 copy.42
  354.6 1.6 copy.43
  356.1 1.6 copy.44
  357.7 3.3 maximum_bitcast_fusion
  (83 shorter events, 7.3 us)
Async XLA Ops:
  6.5 88.1 %all-gather.8.cloned.1.call-start = ((), (), s32[]{:S(2)}) async-start(), calls=%async_computation.1 | async-start | bytes 17436672 | tf_op jit(solution)/shard_map/all_gather | solution.py:71
  7.3 285.4 %all-gather.6.cloned.1.call-start = ((), (), s32[]{:S(2)}) async-start(), calls=%async_computation | async-start | bytes 22282240 | tf_op jit(solution)/shard_map/all_gather | solution.py:17
  115.1 19.6 %copy-start.10 = (f32[4,2816]{1,0:T(4,128)S(1)}, f32[4,2816]{1,0:T(4,128)}, u32[]{:S(2)}) copy-start(f32[4,2816]{1,0:T(4,128)} %param.12) | copy-start | bytes 135172
  115.1 20.5 %copy-start.17 = (f32[2816]{0:T(1024)S(1)}, f32[2816]{0:T(1024)}, u32[]{:S(2)}) copy-start(f32[2816]{0:T(1024)} %param.13) | copy-start | bytes 33796
  131.6 4.0 %collective-permute-start = (bf16[3,2816]{1,0:T(4,128)(2,1)S(1)}, bf16[3,2816]{1,0:T(4,128)(2,1)S(1)}, u32[]{:S(2)}, u32[]{:S(2)}) collective-permute-start(bf16[3,2816]{1,0:T(4,128)(2,1)S(1)} %slice.143), channel_id=1, source_target_pairs={{0,1},{1,2},{2,3},{3,4},{4,5},{5,6},{6,7},{7,8},{8,9},{9,10},{10,1... | collective-permute-start | bytes 50696 | tf_op jit(solution)/shard_map/ppermute | solution.py:12
  134.8 19.5 %copy-start.20 = (f32[40]{0:T(128)}, f32[40]{0:T(128)S(1)}, u32[]{:S(2)}) copy-start(f32[40]{0:T(128)S(1)} %exp.81) | copy-start | bytes 484
  141.9 2.8 copy-start
  146.4 4.4 %copy-start.2 = (bf16[256,2560]{0,1:T(8,128)(2,1)}, bf16[256,2560]{0,1:T(8,128)(2,1)S(1)}, u32[]{:S(2)}) copy-start(bf16[256,2560]{0,1:T(8,128)(2,1)S(1)} %copy.33) | copy-start | bytes 3932164
  150.8 1.9 copy-start.4
  150.8 4.6 %copy-start.6 = (bf16[256,2560]{0,1:T(8,128)(2,1)S(1)}, bf16[256,2560]{0,1:T(8,128)(2,1)}, u32[]{:S(2)}) copy-start(bf16[256,2560]{0,1:T(8,128)(2,1)} %copy.41) | copy-start | bytes 3932164
  154.3 1.0 copy-start.1
  155.4 2.9 copy-start.22
  155.4 39.8 %copy-start.18 = (f32[2560]{0:T(1024)S(1)}, f32[2560]{0:T(1024)}, u32[]{:S(2)}) copy-start(f32[2560]{0:T(1024)} %param.17) | copy-start | bytes 30724
  327.8 2.2 copy-start.19
  331.8 1.8 copy-start.7
  331.8 1.8 copy-start.9
  331.8 1.8 copy-start.15
  331.8 1.8 copy-start.16
  331.8 1.8 copy-start.21
  333.7 5.3 %copy-start.5 = (bf16[256,2560]{0,1:T(8,128)(2,1)S(1)}, bf16[256,2560]{0,1:T(8,128)(2,1)}, u32[]{:S(2)}) copy-start(bf16[256,2560]{0,1:T(8,128)(2,1)} %copy.40) | copy-start | bytes 3932164
  333.7 5.3 %copy-start.13 = (f32[40,256]{1,0:T(8,128)S(1)}, f32[40,256]{1,0:T(8,128)}, u32[]{:S(2)}) copy-start(f32[40,256]{1,0:T(8,128)} %get-tuple-element.143) | copy-start | bytes 122884
  333.7 5.3 %copy-start.14 = (f32[256,40]{0,1:T(8,128)S(1)}, f32[256,40]{0,1:T(8,128)}, u32[]{:S(2)}) copy-start(f32[256,40]{0,1:T(8,128)} %get-tuple-element.152) | copy-start | bytes 122884
  339.0 5.6 %copy-start.3 = (bf16[256,2560]{0,1:T(8,128)(2,1)S(1)}, bf16[256,2560]{0,1:T(8,128)(2,1)}, u32[]{:S(2)}) copy-start(bf16[256,2560]{0,1:T(8,128)(2,1)} %copy-done.2) | copy-start | bytes 3932164
  339.0 5.6 %copy-start.11 = (f32[40,256]{1,0:T(8,128)S(1)}, f32[40,256]{1,0:T(8,128)}, u32[]{:S(2)}) copy-start(f32[40,256]{1,0:T(8,128)} %get-tuple-element.139) | copy-start | bytes 122884
  339.0 5.6 %copy-start.12 = (f32[256,40]{0,1:T(8,128)S(1)}, f32[256,40]{0,1:T(8,128)}, u32[]{:S(2)}) copy-start(f32[256,40]{0,1:T(8,128)} %get-tuple-element.150) | copy-start | bytes 122884
  356.1 1.6 copy-start.8
Sparse Core Ops, SparseCore 0:
  10.4 84.2 all-gather.7
  158.4 134.2 all-gather.5
where the time goes:
time: 370 us; the launch traced here: 368 us
  waiting for transfers between devices  177 us (48%)
  local copies, waits for them, and re-layouts  48.7 us (13%)
  matrix products  47.7 us (13%)
  other arithmetic  42.2 us (11%)
  blocking collectives  34.8 us (9%)
  between operations  14.5 us (4%)
    all_gather x1, waiting for transfers between devices, prefix(): pieces = jax.tree.map(lambda part: lax.all_gather(part, axis), value)  93.6 us
    all_gather x1, waiting for transfers between devices, local(): lax.all_gather(w_xbc, ('dp', 'seq'), axis=0, tiled=True)  81.4 us
    unnamed x1, blocking collectives  34.8 us
    select_n x15, other arithmetic, hop(): jnp.where(position < mine, new, old)  24.3 us
    unnamed x51, local copies, waits for them, and re-layouts  23.3 us
    dot_general x1, matrix products, local(): jnp.dot(token_rows, lax.all_gather(w_xbc, ('dp', 'seq'), axis=0, tiled=Tr...  16.4 us
    dot_general x3, matrix products, block_inner(): jnp.einsum('hij,jhp->ihp', mixing, x_heads, precision=lax.Precision.HIGH)  16 us
    exp x15, local copies, waits for them, and re-layouts, combine_carry(): jnp.exp(later[0])[:, None, None] * earlier[1] + later[1]  10.4 us
  transfers between devices with their start and end apart: 3, of which 3 were waited for; matrix products, arithmetic and copies ran while one was open for 3% of the time, Pallas kernels for 0%

commit v1 on v0

--- a/solution.py
+++ b/solution.py
@@ -68,7 +68,10 @@
     kernel = conv_weight.shape[0]
     projected = jnp.dot(
         token_rows,
-        lax.all_gather(w_xbc, ("dp", "seq"), axis=0, tiled=True),
+        jnp.concatenate(
+            lax.all_to_all(jnp.stack([w_xbc] * lax.axis_size(("dp", "seq"))), ("dp", "seq"), 0, 0),
+            axis=0,
+        ),
         preferred_element_type=jnp.float32,
     )
     xbc = projected.astype(jnp.bfloat16)

time: 370 us -> 527 us (1.42)
  waiting for transfers between devices: 177 us -> 317 us
  starting transfers between devices: 3.15 us -> 13.8 us
    all_to_all x0 -> x1, waiting for transfers between devices: none -> 212 us  [local(): lax.all_to_all(jnp.stack([w_xbc] * lax.axis_size(('dp', 'seq'))), ('dp',...]
    all_gather x1 -> x0, waiting for transfers between devices: 81.4 us -> none  [local(): lax.all_gather(w_xbc, ('dp', 'seq'), axis=0, tiled=True)]
    unnamed x51 -> x58, local copies, waits for them, and re-layouts: 23.3 us -> 1.81 us
    reshape x1 -> x2, local copies, waits for them, and re-layouts: 0.01 us -> 20.5 us  [the longest x1 20.5 us: local(): jnp.concatenate(lax.all_to_all(jnp.stack([w_xbc] * lax.axis_size(('dp', '...]
    all_to_all x0 -> x1, starting transfers between devices: none -> 11.9 us  [local(): lax.all_to_all(jnp.stack([w_xbc] * lax.axis_size(('dp', 'seq'))), ('dp',...]
    all_gather x1, waiting for transfers between devices: 93.6 us -> 105 us  [prefix(): pieces = jax.tree.map(lambda part: lax.all_gather(part, axis), value)]
    another operation x6 -> x7, local copies, waits for them, and re-layouts: 0.34 us -> 7.39 us  [the longest x1 7.05 us: local(): jnp.stack([w_xbc] * lax.axis_size(('dp', 'seq')))]
  transfers between devices with their start and end apart: 3 -> 3, of which waited for: 3 -> 3; matrix products, arithmetic and copies ran while one was open for 3% -> 2% of each run, Pallas kernels for 0% -> 0%
where the time goes in v1:
time: 527 us; the launch traced here: 525 us
  waiting for transfers between devices  317 us (60%)
  local copies, waits for them, and re-layouts  53.4 us (10%)
  matrix products  47.5 us (9%)
  other arithmetic  40.7 us (8%)
  blocking collectives  37 us (7%)
  between operations  14.6 us (3%)
  starting transfers between devices  13.8 us (3%)
    all_to_all x1, waiting for transfers between devices, local(): lax.all_to_all(jnp.stack([w_xbc] * lax.axis_size(('dp', 'seq'))), ('dp',...  212 us
    all_gather x1, waiting for transfers between devices, prefix(): pieces = jax.tree.map(lambda part: lax.all_gather(part, axis), value)  105 us
    unnamed x1, blocking collectives  37 us
    select_n x15, other arithmetic, hop(): jnp.where(position < mine, new, old)  24.3 us
    reshape x1, local copies, waits for them, and re-layouts, local(): jnp.concatenate(lax.all_to_all(jnp.stack([w_xbc] * lax.axis_size(('dp', '...  20.5 us
    dot_general x1, matrix products, local(): jnp.dot(token_rows, jnp.concatenate(lax.all_to_all(jnp.stack([w_xbc] * la...  16.4 us
    dot_general x3, matrix products, block_inner(): jnp.einsum('hij,jhp->ihp', mixing, x_heads, precision=lax.Precision.HIGH)  16 us
    all_to_all x1, starting transfers between devices, local(): lax.all_to_all(jnp.stack([w_xbc] * lax.axis_size(('dp', 'seq'))), ('dp',...  11.9 us
  transfers between devices with their start and end apart: 3, of which 3 were waited for; matrix products, arithmetic and copies ran while one was open for 2% of the time, Pallas kernels for 0%

profile of v1, /device:TPU:1, one launch (start us, length us, event | category | flops | bytes accessed | tf_op | source)
XLA Modules:
  0.0 524.8 jit_solution(882337907588553675)
XLA Ops:
  6.5 7.0 %stack.2 = bf16[128,20,2816]{2,1,0:T(8,128)(2,1)} broadcast(bf16[20,2816]{1,0:T(8,128)(2,1)} %param.11), dimensions={1,2} | broadcast | bytes 14530560 | tf_op jit(solution)/shard_map/stack | solution.py:72
  13.6 11.9 %all-to-all-start = ((bf16[128,20,2816]{2,1,0:T(8,128)(2,1)}), bf16[128,20,2816]{2,1,0:T(8,128)(2,1)}, u32[]{:S(2)}, u32[]{:S(2)}) async-start(bf16[128,20,2816]{2,1,0:T(8,128)(2,1)} %stack.2), calls=%async_computation | async-start | bytes 34603008 | tf_op jit(solution)/shard_map/all_to_all | solution.py:72
  29.2 0.8 fusion.91
  29.9 211.8 %all-to-all-done = bf16[128,20,2816]{2,1,0:T(8,128)(2,1)} async-done(((bf16[128,20,2816]{2,1,0:T(8,128)(2,1)}), bf16[128,20,2816]{2,1,0:T(8,128)(2,1)}, u32[]{:S(2)}, u32[]{:S(2)}) %all-to-all-start) | async-done | bytes 14417952 | tf_op jit(solution)/shard_map/all_to_all | solution.py:72
  241.7 20.5 %reshape.239 = bf16[2560,2816]{1,0:T(8,128)(2,1)} reshape(bf16[128,20,2816]{2,1,0:T(8,128)(2,1)} %all-to-all-done) | data formatting | bytes 28835840 | tf_op jit(solution)/shard_map/reshape | solution.py:71
  262.3 16.4 %convolution_convert_fusion = bf16[768,2816]{1,0:T(8,128)(2,1)S(1)} fusion(bf16[2560,2816]{1,0:T(8,128)(2,1)} %reshape.239, bf16[1,768,2560]{2,1,0:T(8,128)(2,1)} %param.10), kind=kOutput, calls=%fused_computation.42 | convolution fusion | flops 11075125248 | bytes 22675456 | tf_op jit(solution)/shard_map/dot_general | solution.py:69
  278.7 1.9 collective-permute-start
  280.8 0.7 collective-permute-done
  281.5 6.3 %multiply_convert_fusion = bf16[768,2816]{1,0:T(8,128)(2,1)S(1)} fusion(bf16[768,2816]{1,0:T(8,128)(2,1)S(1)} %convolution_convert_fusion, bf16[3,2816]{1,0:T(4,128)(2,1)S(1)} %collective-permute-done, f32[2816]{0:T(1024)S(1)} %get-tuple-element.120, f32[2816]{0:T(1024)S(1)} %get-tuple-element.121, f32[2816]{0:T(1024)S(1)} %get-tuple-element.119, ...), kind=kLoop, calls=%fused_computation.21 | loop fusion | flops 56229888 | bytes 8723968 | tf_op jit(solution)/shard_map/convert_element_type | solution.py:85
  287.8 2.0 fusion.90
  289.8 0.8 copy-done
  290.7 1.6 copy.33
  292.3 1.5 copy.41
  293.8 1.6 copy.40
  295.4 1.9 fusion.42
  297.3 1.8 fusion.40
  299.2 2.9 fusion.52
  303.5 37.0 %all-reduce = f32[640]{0:T(1024)S(1)} all-reduce(f32[640]{0:T(1024)S(1)} %dynamic-update-slice), channel_id=2, replica_groups=mesh['dp'=8,'seq'=16] {'seq'}, use_global_device_ids=true, to_apply=%add | all-reduce | flops 640 | bytes 5120
  341.9 1.1 fusion.83
  343.0 1.1 fusion.76
  344.1 1.1 fusion.73
  345.1 104.8 %all-gather.4.cloned.1.call-done = f32[640,64,128]{2,1,0:T(8,128)} async-done(((f32[40,64,128]{2,1,0:T(8,128)}), f32[640,64,128]{2,1,0:T(8,128)}) %all-gather.4.cloned.1.call-update) | async-done | bytes 20971536 | tf_op jit(solution)/shard_map/all_gather | solution.py:17
  449.9 35.1 %while.14 = (s32[]{:T(128)}, f32[40,64,128]{2,1,0:T(8,128)S(1)}, s32[]{:T(128)}, f32[16,40]{1,0:T(8,128)}, f32[16,40,64,128]{3,2,1,0:T(8,128)}, /*index=5*/s32[]{:T(128)}, s32[]{:T(128)}) while((s32[]{:T(128)}, f32[40,64,128]{2,1,0:T(8,128)S(1)}, s32[]{:T(128)}, f32[16,40]{1,0:T(8,128)}, f32[16,40,64,128]{3,2,1,0:T(8,128)}, ...), condition=%wide.region_7.8_spmd.clone, body=%wide.region_6.7_spmd.clone.sunk | while | flops 1310724 | bytes 3932753 | solution.py:26
  449.9 0.7 exponential_bitcast_fusion.5
  450.6 1.6 fusion.99
  452.2 0.7 exponential_bitcast_fusion.5
  452.9 1.6 fusion.99
  454.6 0.7 exponential_bitcast_fusion.5
  455.3 1.6 fusion.99
  456.9 0.7 exponential_bitcast_fusion.5
  457.6 1.6 fusion.99
  459.2 0.7 exponential_bitcast_fusion.5
  459.9 1.6 fusion.99
  461.6 0.7 exponential_bitcast_fusion.5
  462.2 1.6 fusion.99
  463.9 0.7 exponential_bitcast_fusion.5
  464.6 1.6 fusion.99
  466.2 0.7 exponential_bitcast_fusion.5
  466.9 1.6 fusion.99
  468.5 0.7 exponential_bitcast_fusion.5
  469.2 1.6 fusion.99
  470.9 0.7 exponential_bitcast_fusion.5
  471.6 1.6 fusion.99
  473.2 0.7 exponential_bitcast_fusion.5
  473.9 1.6 fusion.99
  475.5 0.7 exponential_bitcast_fusion.5
  476.2 1.6 fusion.99
  477.9 0.7 exponential_bitcast_fusion.5
  478.5 1.6 fusion.99
  480.2 0.7 exponential_bitcast_fusion.5
  480.9 1.6 fusion.99
  482.5 0.7 exponential_bitcast_fusion.5
  483.2 1.6 fusion.99
  485.0 1.7 fusion.70
  486.8 1.8 fusion.60
  488.7 1.8 fusion.53
  490.6 5.3 %multiply_reduce_fusion.2 = (f32[256,40]{0,1:T(8,128)S(1)}, f32[256,40,64]{0,2,1:T(8,128)S(1)}) fusion(bf16[256,40,64]{0,2,1:T(8,128)(2,1)S(1)} %bitcast.137, f32[40]{0:T(128)S(1)} %copy-done.25, f32[256,40,64]{0,2,1:T(8,128)S(1)} %fusion.70, f32[256,40]{0,1:T(8,128)S(1)} %copy-done.18, f32[40,256]{1,0:T(8,128)S(1)} %copy-done.17, ...), kind=kOutput, calls=%fused_computation.68 | convolution fusion | flops 1021696000 | bytes 7045280 | tf_op jit(solution)/shard_map/hij,jhp->ihp/dot_general | solution.py:52
  496.0 5.5 %multiply_reduce_fusion.1 = (f32[256,40]{0,1:T(8,128)S(1)}, f32[256,40,64]{0,2,1:T(8,128)S(1)}) fusion(bf16[256,40,64]{0,2,1:T(8,128)(2,1)S(1)} %bitcast.135, f32[40]{0:T(128)S(1)} %copy-done.25, f32[256,40,64]{0,2,1:T(8,128)S(1)} %fusion.60, f32[256,40]{0,1:T(8,128)S(1)} %copy-done.16, f32[40,256]{1,0:T(8,128)S(1)} %copy-done.15, ...), kind=kOutput, calls=%fused_computation.66 | convolution fusion | flops 1021696000 | bytes 7045280 | tf_op jit(solution)/shard_map/hij,jhp->ihp/dot_general | solution.py:52
  501.5 5.2 %multiply_reduce_fusion = (f32[256,40]{0,1:T(8,128)S(1)}, f32[256,40,64]{0,2,1:T(8,128)S(1)}) fusion(bf16[256,40,64]{0,2,1:T(8,128)(2,1)S(1)} %bitcast.139, f32[40]{0:T(128)S(1)} %copy-done.25, f32[256,40,64]{0,2,1:T(8,128)S(1)} %fusion.53, f32[256,40]{0,1:T(8,128)S(1)} %copy-done.14, f32[40,256]{1,0:T(8,128)S(1)} %copy-done.13, ...), kind=kOutput, calls=%fused_computation.64 | convolution fusion | flops 1021696000 | bytes 7045280 | tf_op jit(solution)/shard_map/hij,jhp->ihp/dot_general | solution.py:52
  506.8 2.2 multiply_convert_fusion.3
  509.0 2.4 copy.44
  511.5 1.6 copy.43
  513.1 1.6 copy.42
  514.6 3.3 maximum_bitcast_fusion
  (91 shorter events, 6.2 us)
Async XLA Ops:
  13.6 11.9 %copy-start.24 = (f32[40]{0:T(128)S(1)}, f32[40]{0:T(128)}, u32[]{:S(2)}) copy-start(f32[40]{0:T(128)} %param.14) | copy-start | bytes 484
  13.6 12.0 %copy-start.10 = (f32[1,40,768]{2,1,0:T(8,128)S(1)}, f32[1,40,768]{2,1,0:T(8,128)}, u32[]{:S(2)}) copy-start(f32[1,40,768]{2,1,0:T(8,128)} %param.15) | copy-start | bytes 368644
  13.6 228.2 %all-to-all-start = ((bf16[128,20,2816]{2,1,0:T(8,128)(2,1)}), bf16[128,20,2816]{2,1,0:T(8,128)(2,1)}, u32[]{:S(2)}, u32[]{:S(2)}) async-start(bf16[128,20,2816]{2,1,0:T(8,128)(2,1)} %stack.2), calls=%async_computation | async-start | bytes 34603008 | tf_op jit(solution)/shard_map/all_to_all | solution.py:72
  25.5 424.4 %all-gather.4.cloned.1.call-start = ((), (), s32[]{:S(2)}) async-start(), calls=%async_computation.1 | async-start | bytes 22282240 | tf_op jit(solution)/shard_map/all_gather | solution.py:17
  262.2 18.4 %copy-start.12 = (f32[4,2816]{1,0:T(4,128)S(1)}, f32[4,2816]{1,0:T(4,128)}, u32[]{:S(2)}) copy-start(f32[4,2816]{1,0:T(4,128)} %param.12) | copy-start | bytes 135172
  262.2 19.3 %copy-start.19 = (f32[2816]{0:T(1024)S(1)}, f32[2816]{0:T(1024)}, u32[]{:S(2)}) copy-start(f32[2816]{0:T(1024)} %param.13) | copy-start | bytes 33796
  278.7 2.8 collective-permute-start
  280.7 18.4 %copy-start.22 = (f32[40]{0:T(128)}, f32[40]{0:T(128)S(1)}, u32[]{:S(2)}) copy-start(f32[40]{0:T(128)S(1)} %exp.81) | copy-start | bytes 484
  287.8 2.8 copy-start
  292.3 5.1 copy-start.5
  295.4 1.9 copy-start.3
  295.4 3.7 copy-start.7
  297.3 1.8 copy-start.1
  299.2 2.9 copy-start.26
  299.2 42.1 %copy-start.20 = (f32[2560]{0:T(1024)S(1)}, f32[2560]{0:T(1024)}, u32[]{:S(2)}) copy-start(f32[2560]{0:T(1024)} %param.17) | copy-start | bytes 30724
  485.0 1.7 copy-start.21
  486.7 1.9 copy-start.2
  486.7 1.9 copy-start.23
  488.6 1.9 copy-start.6
  488.6 1.9 copy-start.11
  488.6 1.9 copy-start.17
  488.6 1.9 copy-start.18
  488.7 1.9 copy-start.25
  490.6 5.3 %copy-start.4 = (bf16[256,2560]{0,1:T(8,128)(2,1)S(1)}, bf16[256,2560]{0,1:T(8,128)(2,1)}, u32[]{:S(2)}) copy-start(bf16[256,2560]{0,1:T(8,128)(2,1)} %copy-done.3) | copy-start | bytes 3932164
  490.6 5.3 %copy-start.15 = (f32[40,256]{1,0:T(8,128)S(1)}, f32[40,256]{1,0:T(8,128)}, u32[]{:S(2)}) copy-start(f32[40,256]{1,0:T(8,128)} %get-tuple-element.143) | copy-start | bytes 122884
  490.6 5.3 %copy-start.16 = (f32[256,40]{0,1:T(8,128)S(1)}, f32[256,40]{0,1:T(8,128)}, u32[]{:S(2)}) copy-start(f32[256,40]{0,1:T(8,128)} %get-tuple-element.152) | copy-start | bytes 122884
  495.9 5.6 %copy-start.8 = (bf16[256,2560]{0,1:T(8,128)(2,1)S(1)}, bf16[256,2560]{0,1:T(8,128)(2,1)}, u32[]{:S(2)}) copy-start(bf16[256,2560]{0,1:T(8,128)(2,1)} %copy.41) | copy-start | bytes 3932164
  495.9 5.6 %copy-start.13 = (f32[40,256]{1,0:T(8,128)S(1)}, f32[40,256]{1,0:T(8,128)}, u32[]{:S(2)}) copy-start(f32[40,256]{1,0:T(8,128)} %get-tuple-element.142) | copy-start | bytes 122884
  496.0 5.6 %copy-start.14 = (f32[256,40]{0,1:T(8,128)S(1)}, f32[256,40]{0,1:T(8,128)}, u32[]{:S(2)}) copy-start(f32[256,40]{0,1:T(8,128)} %get-tuple-element.151) | copy-start | bytes 122884
  513.1 1.6 copy-start.9
Sparse Core Ops, SparseCore 0:
  302.2 147.6 all-gather.3
